TPU v7x, 256 devices: a whole 4x4x8 slice. The times are simulated.
256 devices in a mesh: orbit: 16 (over y_hi, x, core), tile: 16 (over y_lo, z).
Axes of the slice: x: 4, y: 4 (y_hi: 2, y_lo: 2; y = y_hi * 2 + y_lo), z: 8, core: 2. Of those that a mesh axis runs over, the one named last changes fastest.
Arguments:
- tokens: bfloat16 [64, 1024, 1280], P('orbit', 'tile'), may hold values from -6 to 6
- cotangent: bfloat16 [64, 1024, 1280], P('orbit', 'tile'), may hold values from -60 to 60
- w_query: bfloat16 [1280, 1280], replicated, may hold values from -0.15625 to 0.15625
- w_key: bfloat16 [1280, 1280], replicated, may hold values from -0.15625 to 0.15625
- w_value: bfloat16 [1280, 1280], replicated, may hold values from -0.15625 to 0.15625
- conv_taps: float32 [3, 1280], replicated, may hold values from 0.3 to 1
- conv_bias: float32 [1280], replicated, may hold values from -2 to 2
Outputs:
- grad_tokens: bfloat16 [64, 1024, 1280], P('orbit', 'tile')
All inputs are finite; a program needn't handle non-finite values.
Results may differ from a plain program's by a relative error of at most 0.009.
The roundings to bfloat16 on the way count: a program that leaves them out, or rounds other values in their place, can miss the bound.
Values may be sent and summed in bfloat16 or wider, within the bound.
A program may use at most 64 MiB of HBM per device.

v0:
```python
import math

import jax
import jax.numpy as jnp
from jax import lax
from jax.sharding import PartitionSpec as P

HEAD_DIM = 64


def with_halo(shard, sides, width):
    for axis, dim in sides:
        size, length = (lax.axis_size(axis), shard.shape[dim])
        up = [(i, (i + 1) % size) for i in range(size)]
        down = [(j, i) for i, j in up]
        last = lax.slice_in_dim(shard, length - width, length, axis=dim)
        initial = lax.slice_in_dim(shard, 0, width, axis=dim)
        before = lax.ppermute(last, axis, up)
        after = lax.ppermute(initial, axis, down)
        shard = jnp.concatenate([before, shard, after], axis=dim)
    return shard


def mix_padded(padded, conv_taps, conv_bias):
    source = padded.astype(jnp.float32)
    center = source[1:-1]
    mixed = conv_taps[0] * source[:-2] + conv_taps[1] * center + conv_taps[2] * source[2:]
    return (center + mixed + conv_bias).astype(jnp.bfloat16)


def unmix_padded(padded, conv_taps):
    source = padded.astype(jnp.float32)
    center = source[1:-1]
    return (
        center + conv_taps[0] * source[2:] + conv_taps[1] * center + conv_taps[2] * source[:-2]
    ).astype(jnp.bfloat16)


def project_all(hidden, weights):
    flat_rows = hidden.reshape(-1, hidden.shape[-1])
    return tuple(
        (
            jnp.dot(flat_rows, weight, preferred_element_type=jnp.float32)
            .astype(jnp.bfloat16)
            .reshape(hidden.shape)
            for weight in weights
        )
    )


def back_project(grad_query, grad_key, grad_value, weights):
    full_shape = grad_query.shape
    channels = full_shape[-1]
    total = jnp.dot(
        grad_query.reshape(-1, channels), weights[0].T, preferred_element_type=jnp.float32
    )
    total = total + jnp.dot(
        grad_key.reshape(-1, channels), weights[1].T, preferred_element_type=jnp.float32
    )
    total = total + jnp.dot(
        grad_value.reshape(-1, channels), weights[2].T, preferred_element_type=jnp.float32
    )
    return total.astype(jnp.bfloat16).reshape(full_shape)


def attention_grads(query_rows, key_rows, value_rows, grad_rows):
    frames, tok_count, channels = query_rows.shape
    head_count = channels // HEAD_DIM
    inv_root = 1.0 / math.sqrt(HEAD_DIM)
    shape_heads = (frames, tok_count, head_count, HEAD_DIM)
    q_heads = query_rows.reshape(shape_heads)
    k_heads = key_rows.reshape(shape_heads)
    v_heads = value_rows.reshape(shape_heads)
    g_heads = grad_rows.reshape(shape_heads)
    scores = (
        jnp.einsum("fshd,gshd->shfg", q_heads, k_heads, preferred_element_type=jnp.float32)
        * inv_root
    )
    peak = jnp.max(scores, axis=-1, keepdims=True)
    expo_terms = jnp.exp(scores - peak)
    attn_prob = expo_terms / jnp.sum(expo_terms, axis=-1, keepdims=True)
    prob_low = attn_prob.astype(jnp.bfloat16)
    attn_out = jnp.einsum("shfg,gshd->fshd", prob_low, v_heads, preferred_element_type=jnp.float32)
    row_delta = jnp.sum(g_heads.astype(jnp.float32) * attn_out, axis=-1)
    grad_value = jnp.einsum(
        "shfg,fshd->gshd", prob_low, g_heads, preferred_element_type=jnp.float32
    ).astype(jnp.bfloat16)
    grad_prob = jnp.einsum("fshd,gshd->shfg", g_heads, v_heads, preferred_element_type=jnp.float32)
    d_scores = attn_prob * (grad_prob - jnp.transpose(row_delta, (1, 2, 0))[..., None])
    scores_low = d_scores.astype(jnp.bfloat16)
    grad_query = (
        jnp.einsum("shfg,gshd->fshd", scores_low, k_heads, preferred_element_type=jnp.float32)
        * inv_root
    ).astype(jnp.bfloat16)
    grad_key = (
        jnp.einsum("shfg,fshd->gshd", scores_low, q_heads, preferred_element_type=jnp.float32)
        * inv_root
    ).astype(jnp.bfloat16)
    full_shape = (frames, tok_count, channels)
    return (
        grad_query.reshape(full_shape),
        grad_key.reshape(full_shape),
        grad_value.reshape(full_shape),
    )


def shards(tokens, cotangent, w_query, w_key, w_value, conv_taps, conv_bias):
    frame_rows, tile_rows, channels = tokens.shape
    spatial_all = tile_rows * lax.axis_size("tile")
    grad_f = cotangent.astype(jnp.float32)
    energy = lax.psum(jnp.sum(grad_f * grad_f, axis=(1, 2)), "tile")
    factor = lax.rsqrt(energy / (spatial_all * channels) + 1e-06)
    grad_out = (grad_f * factor[:, None, None]).astype(jnp.bfloat16)
    weights = (w_query, w_key, w_value)
    padded = with_halo(tokens, (("orbit", 0),), 1)
    hidden = mix_padded(padded, conv_taps, conv_bias)
    query_rows, key_rows, value_rows = project_all(hidden, weights)
    query_all, key_all, value_all, grad_all = (
        lax.all_to_all(query_rows, "orbit", split_axis=1, concat_axis=0, tiled=True),
        lax.all_to_all(key_rows, "orbit", split_axis=1, concat_axis=0, tiled=True),
        lax.all_to_all(value_rows, "orbit", split_axis=1, concat_axis=0, tiled=True),
        lax.all_to_all(grad_out, "orbit", split_axis=1, concat_axis=0, tiled=True),
    )
    grad_query, grad_key, grad_value = attention_grads(query_all, key_all, value_all, grad_all)
    grad_query, grad_key, grad_value = (
        lax.all_to_all(grad_query, "orbit", split_axis=0, concat_axis=1, tiled=True),
        lax.all_to_all(grad_key, "orbit", split_axis=0, concat_axis=1, tiled=True),
        lax.all_to_all(grad_value, "orbit", split_axis=0, concat_axis=1, tiled=True),
    )
    grad_hidden = back_project(grad_query, grad_key, grad_value, weights)
    padded_grad = with_halo(grad_hidden, (("orbit", 0),), 1)
    return unmix_padded(padded_grad, conv_taps)


def solution(mesh):
    in_specs = (P("orbit", "tile", None), P("orbit", "tile", None), P(), P(), P(), P(), P())
    out_specs = P("orbit", "tile", None)
    return jax.shard_map(shards, mesh=mesh, in_specs=in_specs, out_specs=out_specs, check_vma=False)
```

profile of v0, /device:TPU:7, one launch (start us, length us, event | category | flops | bytes accessed | tf_op | source)
XLA Modules:
  0.0 230.0 jit_solution(17283773558984169834)
XLA Ops:
  1.9 3.4 %collective-permute-start = (bf16[1,64,1280]{2,1,0:T(8,128)(2,1)}, bf16[1,64,1280]{2,1,0:T(8,128)(2,1)S(1)}, u32[]{:S(2)}, u32[]{:S(2)}) collective-permute-start(bf16[1,64,1280]{2,1,0:T(8,128)(2,1)} %get-tuple-element.10), channel_id=1, source_target_pairs={{0,16},{16,32},{32,48},{48,64},{64,80},{80,96},{96,112},{112,128},... | collective-permute-start | bytes 491528 | tf_op jit(solution)/shard_map/ppermute | solution.py:18
  6.6 29.6 %psum.7 = f32[4]{0:T(128)S(1)} all-reduce(f32[4]{0:T(128)S(1)} %fusion.8), channel_id=1, replica_groups=mesh['orbit'=16,'tile'=16] {'tile'}, use_global_device_ids=true, to_apply=%region_3.0 | all-reduce | flops 4 | bytes 32 | tf_op jit(solution)/shard_map/psum | solution.py:111
  38.9 14.8 %all-to-all-start.2 = ((bf16[4,64,1280]{2,0,1:T(4,128)(2,1)}), bf16[4,64,1280]{2,0,1:T(4,128)(2,1)}, u32[]{:S(2)}, u32[]{:S(2)}) async-start(bf16[4,64,1280]{2,0,1:T(4,128)(2,1)} %copy.110), calls=%async_computation.2 | async-start | bytes 1310720 | tf_op jit(solution)/shard_map/all_to_all | solution.py:122
  59.7 5.4 %all-to-all-done.2 = bf16[4,64,1280]{2,0,1:T(4,128)(2,1)} async-done(((bf16[4,64,1280]{2,0,1:T(4,128)(2,1)}), bf16[4,64,1280]{2,0,1:T(4,128)(2,1)}, u32[]{:S(2)}, u32[]{:S(2)}) %all-to-all-start.2) | async-done | bytes 655392 | tf_op jit(solution)/shard_map/all_to_all | solution.py:122
  65.2 6.6 %all-to-all-start.3 = ((bf16[4,64,1280]{2,0,1:T(4,128)(2,1)}), bf16[4,64,1280]{2,0,1:T(4,128)(2,1)}, u32[]{:S(2)}, u32[]{:S(2)}) async-start(bf16[4,64,1280]{2,0,1:T(4,128)(2,1)} %copy.112), calls=%async_computation.3 | async-start | bytes 1310720 | tf_op jit(solution)/shard_map/all_to_all | solution.py:121
  75.2 8.0 %all-to-all-done.3 = bf16[4,64,1280]{2,0,1:T(4,128)(2,1)} async-done(((bf16[4,64,1280]{2,0,1:T(4,128)(2,1)}), bf16[4,64,1280]{2,0,1:T(4,128)(2,1)}, u32[]{:S(2)}, u32[]{:S(2)}) %all-to-all-start.3) | async-done | bytes 655392 | tf_op jit(solution)/shard_map/all_to_all | solution.py:121
  83.2 6.6 %all-to-all-start.1 = ((bf16[4,64,1280]{2,0,1:T(4,128)(2,1)}), bf16[4,64,1280]{2,0,1:T(4,128)(2,1)}, u32[]{:S(2)}, u32[]{:S(2)}) async-start(bf16[4,64,1280]{2,0,1:T(4,128)(2,1)} %copy.106), calls=%async_computation.1 | async-start | bytes 1310720 | tf_op jit(solution)/shard_map/all_to_all | solution.py:119
  89.8 3.1 %convolution_convert_fusion.2 = bf16[256,1280]{1,0:T(8,128)(2,1)S(1)} fusion(bf16[256,1280]{1,0:T(8,128)(2,1)} %bitcast.76, bf16[1280,1280]{1,0:T(8,128)(2,1)} %param.10), kind=kOutput, calls=%fused_computation.12 | convolution fusion | flops 839188480 | bytes 4587520 | tf_op jit(solution)/shard_map/dot_general | solution.py:43
  94.3 7.0 %all-to-all-done.1 = bf16[4,64,1280]{2,0,1:T(4,128)(2,1)} async-done(((bf16[4,64,1280]{2,0,1:T(4,128)(2,1)}), bf16[4,64,1280]{2,0,1:T(4,128)(2,1)}, u32[]{:S(2)}, u32[]{:S(2)}) %all-to-all-start.1) | async-done | bytes 655392 | tf_op jit(solution)/shard_map/all_to_all | solution.py:119
  101.2 6.6 %all-to-all-start = ((bf16[4,64,1280]{2,0,1:T(4,128)(2,1)}), bf16[4,64,1280]{2,0,1:T(4,128)(2,1)}, u32[]{:S(2)}, u32[]{:S(2)}) async-start(bf16[4,64,1280]{2,0,1:T(4,128)(2,1)} %copy.104), calls=%async_computation | async-start | bytes 1310720 | tf_op jit(solution)/shard_map/all_to_all | solution.py:120
  110.0 3.2 %reshape.67 = bf16[64,4,20,64]{3,2,1,0:T(8,128)(2,1)} reshape(bf16[16,4,4,1280]{3,2,1,0:T(4,128)(2,1)} %bitcast.71) | data formatting | bytes 1310720 | tf_op jit(solution)/shard_map/reshape | solution.py:74
  122.8 3.2 %reshape.64 = bf16[64,4,20,64]{3,2,1,0:T(8,128)(2,1)} reshape(bf16[16,4,4,1280]{3,2,1,0:T(4,128)(2,1)} %copy.105) | data formatting | bytes 1310720 | tf_op jit(solution)/shard_map/reshape | solution.py:72
  129.0 3.2 %reshape.66 = bf16[64,4,20,64]{3,2,1,0:T(8,128)(2,1)} reshape(bf16[16,4,4,1280]{3,2,1,0:T(4,128)(2,1)} %copy.107) | data formatting | bytes 1310720 | tf_op jit(solution)/shard_map/reshape | solution.py:71
  135.2 3.2 %reshape.69 = bf16[64,4,20,64]{3,2,1,0:T(8,128)(2,1)} reshape(bf16[16,4,4,1280]{3,2,1,0:T(4,128)(2,1)} %copy.113) | data formatting | bytes 1310720 | tf_op jit(solution)/shard_map/reshape | solution.py:73
  141.4 4.4 %fusion.27 = (f32[4,20,64]{2,1,0:T(8,128)S(1)}, f32[4,20,64,64]{2,3,1,0:T(8,128)}) fusion(bf16[64,4,20,64]{0,3,2,1:T(8,128)(2,1)} %copy.126, bf16[64,4,20,64]{0,3,2,1:T(8,128)(2,1)} %copy.120), kind=kOutput, calls=%fused_computation.52 | convolution fusion | flops 42926144 | bytes 2641920 | tf_op jit(solution)/shard_map/sub | solution.py:80
  145.8 4.2 %convolution_convert_fusion.3 = bf16[4,20,64,64]{3,2,1,0:T(8,128)(2,1)} fusion(bf16[64,4,20,64]{0,3,2,1:T(8,128)(2,1)} %copy.116, f32[4,20,64,64]{2,3,1,0:T(8,128)} %get-tuple-element.13, f32[4,20,64]{2,1,0:T(8,128)S(1)} %get-tuple-element.12), kind=kOutput, calls=%fused_computation.17 | convolution fusion | flops 42926080 | bytes 2641920 | tf_op jit(solution)/shard_map/shfg,fshd->gshd/dot_general | solution.py:85
  153.1 7.3 %all-to-all-start.6 = ((bf16[64,4,1280]{2,1,0:T(4,128)(2,1)}), bf16[64,4,1280]{2,1,0:T(4,128)(2,1)}, u32[]{:S(2)}, u32[]{:S(2)}) async-start(bf16[64,4,1280]{2,1,0:T(4,128)(2,1)} %copy.134), calls=%async_computation.6 | async-start | bytes 1310720 | tf_op jit(solution)/shard_map/all_to_all | solution.py:128
  160.4 3.4 %multiply_convert_fusion.2 = bf16[4,20,64,64]{2,3,1,0:T(8,128)(2,1)S(1)} fusion(bf16[64,4,20,64]{0,3,2,1:T(8,128)(2,1)} %copy.116, bf16[64,4,20,64]{0,3,2,1:T(8,128)(2,1)} %copy.117, f32[4,20,64]{2,1,0:T(8,128)S(1)} %bitcast.80, f32[4,20,64,64]{2,3,1,0:T(8,128)} %get-tuple-element.13, f32[4,20,64]{2,1,0:T(8,128)S(1)} %get-tuple-element.12), kind=kOutput, calls=%fused_computation.7 | convolution fusion | flops 43253760 | bytes 3317760 | tf_op jit(solution)/shard_map/fshd,gshd->shfg/dot_general | solution.py:88
  166.9 3.2 %reshape.77 = bf16[64,4,1280]{2,1,0:T(4,128)(2,1)} reshape(bf16[64,4,20,64]{3,2,1,0:T(8,128)(2,1)} %copy.143) | data formatting | bytes 1310720 | tf_op jit(solution)/shard_map/reshape | solution.py:101
  171.8 6.6 %all-to-all-start.4 = ((bf16[64,4,1280]{2,1,0:T(4,128)(2,1)}), bf16[64,4,1280]{2,1,0:T(4,128)(2,1)}, u32[]{:S(2)}, u32[]{:S(2)}) async-start(bf16[64,4,1280]{2,1,0:T(4,128)(2,1)} %reshape.77), calls=%async_computation.4 | async-start | bytes 1310720 | tf_op jit(solution)/shard_map/all_to_all | solution.py:126
  183.0 3.2 %reshape.78 = bf16[64,4,1280]{2,1,0:T(4,128)(2,1)} reshape(bf16[64,4,20,64]{3,2,1,0:T(8,128)(2,1)} %copy.144) | data formatting | bytes 1310720 | tf_op jit(solution)/shard_map/reshape | solution.py:102
  186.2 3.6 %all-to-all-done.4 = bf16[64,4,1280]{2,1,0:T(4,128)(2,1)} async-done(((bf16[64,4,1280]{2,1,0:T(4,128)(2,1)}), bf16[64,4,1280]{2,1,0:T(4,128)(2,1)}, u32[]{:S(2)}, u32[]{:S(2)}) %all-to-all-start.4) | async-done | bytes 655392 | tf_op jit(solution)/shard_map/all_to_all | solution.py:126
  189.9 6.6 %all-to-all-start.5 = ((bf16[64,4,1280]{2,1,0:T(4,128)(2,1)}), bf16[64,4,1280]{2,1,0:T(4,128)(2,1)}, u32[]{:S(2)}, u32[]{:S(2)}) async-start(bf16[64,4,1280]{2,1,0:T(4,128)(2,1)} %reshape.78), calls=%async_computation.5 | async-start | bytes 1310720 | tf_op jit(solution)/shard_map/all_to_all | solution.py:127
  222.6 6.1 %collective-permute-done.3 = bf16[1,64,1280]{2,1,0:T(8,128)(2,1)S(1)} collective-permute-done((bf16[1,64,1280]{2,1,0:T(8,128)(2,1)S(1)}, bf16[1,64,1280]{2,1,0:T(8,128)(2,1)S(1)}, u32[]{:S(2)}, u32[]{:S(2)}) %collective-permute-start.3) | collective-permute-done | bytes 163872 | tf_op jit(solution)/shard_map/ppermute | solution.py:19
  (76 shorter events, 77.3 us)
Async XLA Ops:
  0.0 71.7 %copy-start = (bf16[1280,1280]{1,0:T(8,128)(2,1)S(1)}, bf16[1280,1280]{1,0:T(8,128)(2,1)}, u32[]{:S(2)}) copy-start(bf16[1280,1280]{1,0:T(8,128)(2,1)} %param.9) | copy-start | bytes 9830404
  1.9 51.9 %collective-permute-start = (bf16[1,64,1280]{2,1,0:T(8,128)(2,1)}, bf16[1,64,1280]{2,1,0:T(8,128)(2,1)S(1)}, u32[]{:S(2)}, u32[]{:S(2)}) collective-permute-start(bf16[1,64,1280]{2,1,0:T(8,128)(2,1)} %get-tuple-element.10), channel_id=1, source_target_pairs={{0,16},{16,32},{32,48},{48,64},{64,80},{80,96},{96,112},{112,128},... | collective-permute-start | bytes 491528 | tf_op jit(solution)/shard_map/ppermute | solution.py:18
  6.6 47.2 %collective-permute-start.1 = (bf16[1,64,1280]{2,1,0:T(8,128)(2,1)}, bf16[1,64,1280]{2,1,0:T(8,128)(2,1)}, u32[]{:S(2)}, u32[]{:S(2)}) collective-permute-start(bf16[1,64,1280]{2,1,0:T(8,128)(2,1)} %get-tuple-element.11), channel_id=1, source_target_pairs={{16,0},{32,16},{48,32},{64,48},{80,64},{96,80},{112,96},{128,112},... | collective-permute-start | bytes 491528 | tf_op jit(solution)/shard_map/ppermute | solution.py:19
  37.6 16.2 %copy-start.10 = (f32[3,1280]{1,0:T(4,128)S(1)}, f32[3,1280]{1,0:T(4,128)}, u32[]{:S(2)}) copy-start(f32[3,1280]{1,0:T(4,128)} %param.12) | copy-start | bytes 46084
  38.9 26.2 %all-to-all-start.2 = ((bf16[4,64,1280]{2,0,1:T(4,128)(2,1)}), bf16[4,64,1280]{2,0,1:T(4,128)(2,1)}, u32[]{:S(2)}, u32[]{:S(2)}) async-start(bf16[4,64,1280]{2,0,1:T(4,128)(2,1)} %copy.110), calls=%async_computation.2 | async-start | bytes 1310720 | tf_op jit(solution)/shard_map/all_to_all | solution.py:122
  53.8 1.4 copy-start.11
  55.2 2.2 copy-start.12
  55.5 2.8 %copy-start.8 = (bf16[4,64,1280]{2,1,0:T(8,128)(2,1)}, bf16[4,64,1280]{2,1,0:T(8,128)(2,1)S(1)}, u32[]{:S(2)}) copy-start(bf16[4,64,1280]{2,1,0:T(8,128)(2,1)S(1)} %fusion.17) | copy-start | bytes 1966084
  65.2 18.0 %all-to-all-start.3 = ((bf16[4,64,1280]{2,0,1:T(4,128)(2,1)}), bf16[4,64,1280]{2,0,1:T(4,128)(2,1)}, u32[]{:S(2)}, u32[]{:S(2)}) async-start(bf16[4,64,1280]{2,0,1:T(4,128)(2,1)} %copy.112), calls=%async_computation.3 | async-start | bytes 1310720 | tf_op jit(solution)/shard_map/all_to_all | solution.py:121
  83.2 18.0 %all-to-all-start.1 = ((bf16[4,64,1280]{2,0,1:T(4,128)(2,1)}), bf16[4,64,1280]{2,0,1:T(4,128)(2,1)}, u32[]{:S(2)}, u32[]{:S(2)}) async-start(bf16[4,64,1280]{2,0,1:T(4,128)(2,1)} %copy.106), calls=%async_computation.1 | async-start | bytes 1310720 | tf_op jit(solution)/shard_map/all_to_all | solution.py:119
  101.2 19.4 %all-to-all-start = ((bf16[4,64,1280]{2,0,1:T(4,128)(2,1)}), bf16[4,64,1280]{2,0,1:T(4,128)(2,1)}, u32[]{:S(2)}, u32[]{:S(2)}) async-start(bf16[4,64,1280]{2,0,1:T(4,128)(2,1)} %copy.104), calls=%async_computation | async-start | bytes 1310720 | tf_op jit(solution)/shard_map/all_to_all | solution.py:120
  145.8 4.2 %copy-start.4 = (f32[4,20,64,64]{2,3,1,0:T(8,128)S(1)}, f32[4,20,64,64]{2,3,1,0:T(8,128)}, u32[]{:S(2)}) copy-start(f32[4,20,64,64]{2,3,1,0:T(8,128)} %get-tuple-element.13) | copy-start | bytes 3932164
  145.8 4.2 %copy-start.6 = (bf16[64,4,20,64]{0,3,2,1:T(8,128)(2,1)S(1)}, bf16[64,4,20,64]{0,3,2,1:T(8,128)(2,1)}, u32[]{:S(2)}) copy-start(bf16[64,4,20,64]{0,3,2,1:T(8,128)(2,1)} %copy.116) | copy-start | bytes 1966084
  145.8 4.2 %copy-start.7 = (bf16[64,4,20,64]{0,3,2,1:T(8,128)(2,1)S(1)}, bf16[64,4,20,64]{0,3,2,1:T(8,128)(2,1)}, u32[]{:S(2)}) copy-start(bf16[64,4,20,64]{0,3,2,1:T(8,128)(2,1)} %copy.117) | copy-start | bytes 1966084
  153.1 18.7 %all-to-all-start.6 = ((bf16[64,4,1280]{2,1,0:T(4,128)(2,1)}), bf16[64,4,1280]{2,1,0:T(4,128)(2,1)}, u32[]{:S(2)}, u32[]{:S(2)}) async-start(bf16[64,4,1280]{2,1,0:T(4,128)(2,1)} %copy.134), calls=%async_computation.6 | async-start | bytes 1310720 | tf_op jit(solution)/shard_map/all_to_all | solution.py:128
  160.4 3.4 %copy-start.1 = (bf16[64,4,20,64]{0,3,2,1:T(8,128)(2,1)S(1)}, bf16[64,4,20,64]{0,3,2,1:T(8,128)(2,1)}, u32[]{:S(2)}) copy-start(bf16[64,4,20,64]{0,3,2,1:T(8,128)(2,1)} %copy.120) | copy-start | bytes 1966084
  171.8 18.0 %all-to-all-start.4 = ((bf16[64,4,1280]{2,1,0:T(4,128)(2,1)}), bf16[64,4,1280]{2,1,0:T(4,128)(2,1)}, u32[]{:S(2)}, u32[]{:S(2)}) async-start(bf16[64,4,1280]{2,1,0:T(4,128)(2,1)} %reshape.77), calls=%async_computation.4 | async-start | bytes 1310720 | tf_op jit(solution)/shard_map/all_to_all | solution.py:126
  189.9 18.1 %all-to-all-start.5 = ((bf16[64,4,1280]{2,1,0:T(4,128)(2,1)}), bf16[64,4,1280]{2,1,0:T(4,128)(2,1)}, u32[]{:S(2)}, u32[]{:S(2)}) async-start(bf16[64,4,1280]{2,1,0:T(4,128)(2,1)} %reshape.78), calls=%async_computation.5 | async-start | bytes 1310720 | tf_op jit(solution)/shard_map/all_to_all | solution.py:127
  212.3 2.3 copy-start.3
  212.3 2.3 %copy-start.5 = (bf16[256,1280]{1,0:T(8,128)(2,1)S(1)}, bf16[256,1280]{1,0:T(8,128)(2,1)}, u32[]{:S(2)}) copy-start(bf16[256,1280]{1,0:T(8,128)(2,1)} %reshape.73) | copy-start | bytes 1966084
  214.6 1.1 copy-start.9
  214.6 2.1 copy-start.13
  217.8 4.8 %collective-permute-start.2 = (bf16[1,64,1280]{2,1,0:T(8,128)(2,1)S(1)}, bf16[1,64,1280]{2,1,0:T(8,128)(2,1)S(1)}, u32[]{:S(2)}, u32[]{:S(2)}) collective-permute-start(bf16[1,64,1280]{2,1,0:T(8,128)(2,1)S(1)} %get-tuple-element.8), channel_id=1, source_target_pairs={{0,16},{16,32},{32,48},{48,64},{64,80},{80,96},{96,112},{112,128},... | collective-permute-start | bytes 491528 | tf_op jit(solution)/shard_map/ppermute | solution.py:18
  220.4 8.4 %collective-permute-start.3 = (bf16[1,64,1280]{2,1,0:T(8,128)(2,1)S(1)}, bf16[1,64,1280]{2,1,0:T(8,128)(2,1)S(1)}, u32[]{:S(2)}, u32[]{:S(2)}) collective-permute-start(bf16[1,64,1280]{2,1,0:T(8,128)(2,1)S(1)} %get-tuple-element.9), channel_id=1, source_target_pairs={{16,0},{32,16},{48,32},{64,48},{80,64},{96,80},{112,96},{128,112},... | collective-permute-start | bytes 491528 | tf_op jit(solution)/shard_map/ppermute | solution.py:19
  (1 other events, 1.1 us)
where the time goes:
time: 232 us; the launch traced here: 230 us
  local copies, waits for them, and re-layouts  70.1 us (30%)
  starting transfers between devices  61 us (26%)
  waiting for transfers between devices  36.7 us (16%)
  blocking collectives  29.6 us (13%)
  matrix products  26.7 us (12%)
  other arithmetic  5.57 us (2%)
    psum x1, blocking collectives, shards(): energy = lax.psum(jnp.sum(grad_f * grad_f, axis=(1, 2)), 'tile')  29.6 us
    all_to_all x1, starting transfers between devices, shards(): lax.all_to_all(grad_out, 'orbit', split_axis=1, concat_axis=0, tiled=True)  14.8 us
    all_to_all x1, waiting for transfers between devices, shards(): lax.all_to_all(value_rows, 'orbit', split_axis=1, concat_axis=0, tiled=True)  7.96 us
    all_to_all x1, starting transfers between devices, shards(): lax.all_to_all(grad_value, 'orbit', split_axis=0, concat_axis=1, tiled=True)  7.27 us
    all_to_all x1, waiting for transfers between devices, shards(): lax.all_to_all(query_rows, 'orbit', split_axis=1, concat_axis=0, tiled=True)  6.95 us
    all_to_all x1, starting transfers between devices, shards(): lax.all_to_all(key_rows, 'orbit', split_axis=1, concat_axis=0, tiled=True)  6.61 us
    all_to_all x1, starting transfers between devices, shards(): lax.all_to_all(grad_key, 'orbit', split_axis=0, concat_axis=1, tiled=True)  6.6 us
    all_to_all x1, starting transfers between devices, shards(): lax.all_to_all(query_rows, 'orbit', split_axis=1, concat_axis=0, tiled=True)  6.59 us
  transfers between devices with their start and end apart: 11, of which 8 were waited for; matrix products, arithmetic and copies ran while one was open for 24% of the time, Pallas kernels for 0%

commit v1 on v0

v1 whole, which is shorter than its diff:
```python
import functools

import jax
import jax.numpy as jnp
from jax import lax
from jax.experimental import pallas as pl
from jax.experimental.pallas import tpu as pltpu
from jax.sharding import PartitionSpec as P

MESH = pl.DeviceIdType.MESH
HEAD_DIM = 64
PAIR = 2 * HEAD_DIM
SCALE = HEAD_DIM**-0.5
GROUP = 16
HALVES = 2
CHUNK = 8
ROWS = GROUP * CHUNK
BF16 = jnp.bfloat16
F32 = jnp.float32


def partner_of(me, k):
    core, x, y = me % 2, (me // 2) % 4, me // 8
    return ((y + k // 8) % 2) * 8 + ((x + (k // 2) % 4) % 4) * 2 + (core + k % 2) % 2


def source_of(me, k):
    core, x, y = me % 2, (me // 2) % 4, me // 8
    return ((y + k // 8) % 2) * 8 + ((x + 4 - (k // 2) % 4) % 4) * 2 + (core + k % 2) % 2


def one_hot(source):
    columns = lax.broadcasted_iota(jnp.int32, (ROWS, ROWS), 1)
    return jnp.where(columns == source, 1.0, 0.0).astype(BF16)


def row_index():
    return lax.broadcasted_iota(jnp.int32, (ROWS, ROWS), 0)


def dot(a, b, dims=((1,), (0,))):
    return lax.dot_general(a, b, (dims, ((), ())), preferred_element_type=F32)


def stacked(block):
    lanes = lax.broadcasted_iota(jnp.int32, block.shape, 1)
    zero = jnp.zeros_like(block)
    return jnp.concatenate(
        [jnp.where(lanes < HEAD_DIM, block, zero), jnp.where(lanes < HEAD_DIM, zero, block)], axis=0
    )


def kernel(
    comm,
    tokens_hbm,
    cot_hbm,
    wq_hbm,
    wk_hbm,
    wv_hbm,
    taps_ref,
    bias_ref,
    out_ref,
    tok_in,
    cot_in,
    w,
    tsend,
    trecv,
    csend,
    crecv,
    gsend,
    grecv,
    esend,
    erecv,
    fsend,
    frecv,
    hid,
    qkv,
    qs_all,
    probs,
    grads,
    ghid,
    load_sem,
    send_sem,
    recv_sem,
):
    me = lax.axis_index("orbit")
    tile = lax.axis_index("tile")
    channels = tok_in.shape[-1]
    barrier = pltpu.get_barrier_semaphore()
    if comm:
        for k in range(1, GROUP):
            pl.semaphore_signal(barrier, inc=1, device_id=((me + k) % GROUP, tile), device_id_type=MESH)
            pl.semaphore_signal(barrier, inc=1, device_id=(me, (tile + k) % GROUP), device_id_type=MESH)
    loads = [
        pltpu.make_async_copy(tokens_hbm, tok_in, load_sem.at[0]),
        pltpu.make_async_copy(cot_hbm, cot_in, load_sem.at[1]),
        pltpu.make_async_copy(wq_hbm, w.at[0], load_sem.at[2]),
        pltpu.make_async_copy(wk_hbm, w.at[1], load_sem.at[3]),
        pltpu.make_async_copy(wv_hbm, w.at[2], load_sem.at[4]),
    ]
    for load in loads:
        load.start()

    rows = row_index()
    half_tokens = tok_in.shape[1] // HALVES
    to_chunks = one_hot((rows & 3) * half_tokens + (rows >> 3) * 2 + ((rows >> 2) & 1))
    from_chunks = one_hot(((rows % half_tokens) >> 1) * CHUNK + (rows & 1) * 4 + rows // half_tokens)
    before = one_hot((rows + ROWS - jnp.where((rows & 3) == 0, 5, 1)) % ROWS)
    after = one_hot((rows + jnp.where((rows & 3) == 3, 5, 1)) % ROWS)

    def pack(src, dst, h):
        flat = src[:, pl.ds(h * half_tokens, half_tokens), :].reshape(ROWS, channels)
        dst[h] = dot(to_chunks, flat).astype(BF16).reshape(GROUP, CHUNK, channels)

    def exchange_copy(a, src, dst, h, k):
        to = partner_of(me, k)
        return pltpu.make_async_remote_copy(
            src_ref=src.at[h, to],
            dst_ref=dst.at[h, me],
            send_sem=send_sem.at[a, k],
            recv_sem=recv_sem.at[a, k],
            device_id=(to, tile),
            device_id_type=MESH,
        )

    def arrival(a, src, dst, h, k):
        origin = source_of(me, k)
        return pltpu.make_async_remote_copy(
            src_ref=src.at[h, origin],
            dst_ref=dst.at[h, origin],
            send_sem=send_sem.at[a, k],
            recv_sem=recv_sem.at[a, k],
            device_id=(origin, tile),
            device_id_type=MESH,
        )

    def send(a, src, dst, h):
        if comm:
            for k in range(GROUP - 1, 0, -1):
                exchange_copy(a, src, dst, h, k).start()
        dst[h, me] = src[h, me]

    def receive(a, src, dst, h):
        if comm:
            for k in range(GROUP - 1, 0, -1):
                arrival(a, src, dst, h, k).wait_recv()

    def small_copy(a, src, dst, slot, k, to):
        return pltpu.make_async_remote_copy(
            src_ref=src,
            dst_ref=dst.at[slot],
            send_sem=send_sem.at[a, k],
            recv_sem=recv_sem.at[a, k],
            device_id=to,
            device_id_type=MESH,
        )

    loads[0].wait()
    pack(tok_in, tsend, 0)
    loads[1].wait()
    parts = []
    for f in range(cot_in.shape[0]):
        frame = cot_in[f].astype(F32)
        parts.append(jnp.sum(frame * frame, axis=0, keepdims=True))
    squares = jnp.concatenate(parts + parts, axis=0)
    lanes_sum = squares[:, :128]
    for c in range(128, channels, 128):
        lanes_sum = lanes_sum + squares[:, c : c + 128]
    esend[...] = lanes_sum
    if comm:
        pl.semaphore_wait(barrier, 2 * (GROUP - 1))
        for k in range(1, GROUP):
            small_copy(6, esend, erecv, tile, k, (me, (tile + k) % GROUP)).start()
    erecv[tile] = esend[...]
    send(0, tsend, trecv, 0)
    pack(tok_in, tsend, 1)
    send(1, tsend, trecv, 1)
    pack(cot_in, csend, 0)
    if comm:
        for k in range(1, GROUP):
            small_copy(6, esend, erecv, (tile + GROUP - k) % GROUP, k, (me, (tile + k) % GROUP)).wait_recv()
    energy = erecv[0]
    for t in range(1, GROUP):
        energy = energy + erecv[t]
    energy = jnp.sum(energy, axis=1, keepdims=True)
    count = tok_in.shape[1] * GROUP * channels
    fsend[...] = jnp.broadcast_to(lax.rsqrt(energy / count + 1e-06), fsend.shape)
    if comm:
        for k in range(1, GROUP):
            small_copy(7, fsend, frecv, me, k, (partner_of(me, k), tile)).start()
    frecv[me] = fsend[...]
    send(2, csend, crecv, 0)
    pack(cot_in, csend, 1)
    send(3, csend, crecv, 1)

    same_token = ((row_index() >> 2) & 1) == ((lax.broadcasted_iota(jnp.int32, (ROWS, ROWS), 1) >> 2) & 1)
    closed = jnp.where(same_token, 0.0, -1e30).astype(F32)
    closed = jnp.concatenate([closed, closed], axis=1)
    step = 256

    for h in range(HALVES):
        receive(h, tsend, trecv, h)
        for c in range(0, channels, step):
            cols = slice(c, c + step)
            x = trecv[h, :, :, cols].reshape(ROWS, step)
            prev, succ, here = dot(before, x), dot(after, x), x.astype(F32)
            mixed = taps_ref[0:1, cols] * prev + taps_ref[1:2, cols] * here + taps_ref[2:3, cols] * succ
            hid[h, :, cols] = (here + mixed + bias_ref[:, cols]).astype(BF16)
        if h == 0:
            for load in loads[2:]:
                load.wait()
        for i in range(3):
            for c in range(0, channels, step):
                cols = slice(c, c + step)
                block = dot(hid[h], w[i, :, cols])
                if i == 0:
                    block = block * SCALE
                qkv[i, h, :, cols] = block.astype(BF16)
        for m in range(channels // PAIR):
            cols = slice(m * PAIR, (m + 1) * PAIR)
            qs = stacked(qkv[0, h, :, cols])
            qs_all[h, m] = qs
            scores = dot(qkv[1, h, :, cols], qs, ((1,), (1,))) + closed
            expo = jnp.exp(scores - jnp.max(scores, axis=0, keepdims=True))
            probs[h, m] = expo / jnp.sum(expo, axis=0, keepdims=True)

    for h in range(HALVES):
        if comm and h == 0:
            for k in range(1, GROUP):
                small_copy(7, fsend, frecv, source_of(me, k), k, (source_of(me, k), tile)).wait_recv()
        receive(2 + h, csend, crecv, h)
        factor = frecv[...].reshape(ROWS, 128)
        for m in range(channels // PAIR):
            cols = slice(m * PAIR, (m + 1) * PAIR)
            grad_out = (crecv[h, :, :, cols].reshape(ROWS, PAIR).astype(F32) * factor).astype(BF16)
            gs = stacked(grad_out)
            grad_prob = dot(qkv[2, h, :, cols], gs, ((1,), (1,)))
            prob = probs[h, m]
            low = prob.astype(BF16)
            delta = jnp.sum(low.astype(F32) * grad_prob, axis=0, keepdims=True)
            grad_scores = (prob * (grad_prob - delta)).astype(BF16)
            grads[2, h, :, cols] = dot(low, gs).astype(BF16)
            grads[1, h, :, cols] = dot(grad_scores, qs_all[h, m]).astype(BF16)
            both = dot(grad_scores, qkv[1, h, :, cols], ((0,), (0,)))
            lanes = lax.broadcasted_iota(jnp.int32, (ROWS, PAIR), 1)
            grads[0, h, :, cols] = (jnp.where(lanes < HEAD_DIM, both[:ROWS], both[ROWS:]) * SCALE).astype(BF16)
        for c in range(0, channels, step):
            cols = slice(c, c + step)
            total = dot(grads[0, h], w[0, cols, :], ((1,), (1,)))
            total = total + dot(grads[1, h], w[1, cols, :], ((1,), (1,)))
            total = total + dot(grads[2, h], w[2, cols, :], ((1,), (1,)))
            x = total.astype(BF16)
            prev, succ, here = dot(before, x), dot(after, x), x.astype(F32)
            back = here + taps_ref[0:1, cols] * succ + taps_ref[1:2, cols] * here + taps_ref[2:3, cols] * prev
            gsend[h, :, :, cols] = back.astype(BF16).reshape(GROUP, CHUNK, step)
        send(4 + h, gsend, grecv, h)

    for h in range(HALVES):
        receive(4 + h, gsend, grecv, h)
        flat = dot(from_chunks, grecv[h].reshape(ROWS, channels)).astype(BF16)
        out_ref[:, pl.ds(h * half_tokens, half_tokens), :] = flat.reshape(out_ref.shape[0], half_tokens, channels)

    if comm:
        for h in range(HALVES):
            for a, src, dst in ((0, tsend, trecv), (2, csend, crecv), (4, gsend, grecv)):
                for k in range(GROUP - 1, 0, -1):
                    exchange_copy(a + h, src, dst, h, k).wait_send()
        for k in range(1, GROUP):
            small_copy(6, esend, erecv, tile, k, (me, (tile + k) % GROUP)).wait_send()
            small_copy(7, fsend, frecv, me, k, (partner_of(me, k), tile)).wait_send()


def shards(comm, tokens, cotangent, w_query, w_key, w_value, conv_taps, conv_bias):
    frames, toks, channels = tokens.shape
    pairs = channels // PAIR
    exchange = pltpu.VMEM((HALVES, GROUP, CHUNK, channels), BF16)
    hbm, vmem = pl.BlockSpec(memory_space=pl.ANY), pl.BlockSpec(memory_space=pltpu.VMEM)
    return pl.pallas_call(
        functools.partial(kernel, comm),
        out_shape=jax.ShapeDtypeStruct((frames, toks, channels), BF16),
        in_specs=[hbm, hbm, hbm, hbm, hbm, vmem, vmem],
        out_specs=vmem,
        scratch_shapes=[
            pltpu.VMEM((frames, toks, channels), BF16),
            pltpu.VMEM((frames, toks, channels), BF16),
            pltpu.VMEM((3, channels, channels), BF16),
            exchange,
            exchange,
            exchange,
            exchange,
            exchange,
            exchange,
            pltpu.VMEM((8, 128), F32),
            pltpu.VMEM((GROUP, 8, 128), F32),
            pltpu.VMEM((8, 128), F32),
            pltpu.VMEM((GROUP, 8, 128), F32),
            pltpu.VMEM((HALVES, ROWS, channels), BF16),
            pltpu.VMEM((3, HALVES, ROWS, channels), BF16),
            pltpu.VMEM((HALVES, pairs, 2 * ROWS, PAIR), BF16),
            pltpu.VMEM((HALVES, pairs, ROWS, 2 * ROWS), F32),
            pltpu.VMEM((3, HALVES, ROWS, channels), BF16),
            pltpu.VMEM((8, 128), BF16),
            pltpu.SemaphoreType.DMA((5,)),
            pltpu.SemaphoreType.DMA((8, GROUP)),
            pltpu.SemaphoreType.DMA((8, GROUP)),
        ],
        compiler_params=pltpu.CompilerParams(
            collective_id=0, has_side_effects=True, vmem_limit_bytes=56 << 20
        ),
    )(tokens, cotangent, w_query, w_key, w_value, conv_taps, conv_bias.reshape(1, channels))


def solution(mesh, comm=True):
    in_specs = (P("orbit", "tile", None), P("orbit", "tile", None), P(), P(), P(), P(), P())
    out_specs = P("orbit", "tile", None)
    return jax.shard_map(
        functools.partial(shards, comm), mesh=mesh, in_specs=in_specs, out_specs=out_specs, check_vma=False
    )
```

time: 232 us -> 57.7 us (0.25)
  the two profiles are of different devices: /device:TPU:7 before, /device:TPU:1 now
where the time goes in v1:
time: 57.7 us; the launch traced here: 57.5 us
  Pallas kernels  54.3 us (94%)
  local copies, waits for them, and re-layouts  3.26 us (6%)
    pallas_call x1, Pallas kernels, shards(): pl.pallas_call(functools.partial(kernel, comm), out_shape=jax.ShapeDtypeS...  54.3 us
    unnamed x1, local copies, waits for them, and re-layouts  1.97 us
    reshape x1, local copies, waits for them, and re-layouts, shards(): conv_bias.reshape(1, channels)  1.29 us

profile of v1, /device:TPU:1, one launch (start us, length us, event | category | flops | bytes accessed | tf_op | source)
XLA Modules:
  0.0 57.5 jit_solution(16231378010231772316)
XLA Ops:
  0.0 1.3 %reshape.3.bias_ref = f32[1,1280]{1,0:T(1,128)} reshape(f32[1280]{0:T(1024)} %param.13) | data formatting | bytes 10240 | tf_op jit(solution)/shard_map/reshape | solution.py:310
  1.3 54.3 %shard_map.73 = bf16[4,64,1280]{2,1,0:T(8,128)(2,1)} custom-call(bf16[4,64,1280]{2,1,0:T(8,128)(2,1)} %tokens_hbm.1, bf16[4,64,1280]{2,1,0:T(8,128)(2,1)} %cot_hbm.1, bf16[1280,1280]{1,0:T(8,128)(2,1)} %wq_hbm.1, bf16[1280,1280]{1,0:T(8,128)(2,1)} %wk_hbm.1, bf16[1280,1280]{1,0:T(8,128)(2,1)} %wv_hbm.1, f32[3,1280]{1,0:T(4,128)} %taps_ref.1, ...), custom_call_target="tpu_custom_call" | custom-call | tf_op jit(solution)/shard_map/pallas_call | solution.py:278
  55.6 2.0 %copy.9 = bf16[4,64,1280]{2,1,0:T(8,128)(2,1)} copy(bf16[4,64,1280]{2,1,0:T(8,128)(2,1)} %shard_map.73) | data formatting | bytes 1310720

commit v2 on v1

v2 whole, which is shorter than its diff:
```python
import functools

import jax
import jax.numpy as jnp
from jax import lax
from jax.experimental import pallas as pl
from jax.experimental.pallas import tpu as pltpu
from jax.sharding import PartitionSpec as P

MESH = pl.DeviceIdType.MESH
HEAD_DIM = 64
PAIR = 2 * HEAD_DIM
SCALE = HEAD_DIM**-0.5
GROUP = 16
HALVES = 2
CHUNK = 8
HUB = 1
SPLITS = ((0, 768), (768, 1280))
ROWS = GROUP * CHUNK
BF16 = jnp.bfloat16
F32 = jnp.float32


def partner_of(me, k):
    core, x, y = me % 2, (me // 2) % 4, me // 8
    return ((y + k // 8) % 2) * 8 + ((x + (k // 2) % 4) % 4) * 2 + (core + k % 2) % 2


def source_of(me, k):
    core, x, y = me % 2, (me // 2) % 4, me // 8
    return ((y + k // 8) % 2) * 8 + ((x + 4 - (k // 2) % 4) % 4) * 2 + (core + k % 2) % 2


def one_hot(source):
    columns = lax.broadcasted_iota(jnp.int32, (ROWS, ROWS), 1)
    return jnp.where(columns == source, 1.0, 0.0).astype(BF16)


def row_index():
    return lax.broadcasted_iota(jnp.int32, (ROWS, ROWS), 0)


def dot(a, b, dims=((1,), (0,))):
    return lax.dot_general(a, b, (dims, ((), ())), preferred_element_type=F32)


def stacked(block):
    lanes = lax.broadcasted_iota(jnp.int32, block.shape, 1)
    zero = jnp.zeros_like(block)
    return jnp.concatenate(
        [jnp.where(lanes < HEAD_DIM, block, zero), jnp.where(lanes < HEAD_DIM, zero, block)], axis=0
    )


def kernel(
    comm,
    tokens_hbm,
    cot_hbm,
    wq_hbm,
    wk_hbm,
    wv_hbm,
    taps_ref,
    bias_ref,
    out_ref,
    tok_in,
    cot_in,
    w,
    wt,
    tsend,
    trecv,
    csend,
    crecv,
    gsend,
    grecv,
    esend,
    erecv,
    hsend,
    hrecv,
    fsend,
    frecv,
    hid,
    qkv,
    qs_all,
    probs,
    grads,
    load_sem,
    send_sem,
    recv_sem,
    small_send,
    small_recv,
    go_sem,
):
    me = lax.axis_index("orbit")
    tile = lax.axis_index("tile")
    channels = tok_in.shape[-1]
    barrier = pltpu.get_barrier_semaphore()

    pending = []

    def launch(copy):
        copy.start()
        pending.append(copy)

    def drain():
        for copy in pending:
            copy.wait_send()

    loads = [
        pltpu.make_async_copy(tokens_hbm, tok_in, load_sem.at[0]),
        pltpu.make_async_copy(cot_hbm, cot_in, load_sem.at[1]),
        pltpu.make_async_copy(wq_hbm, w.at[0], load_sem.at[2]),
        pltpu.make_async_copy(wk_hbm, w.at[1], load_sem.at[3]),
        pltpu.make_async_copy(wv_hbm, w.at[2], load_sem.at[4]),
    ]
    for load in loads[:2]:
        load.start()
    if comm:
        for k in range(1, GROUP):
            peer = (me + k) % GROUP

            @pl.when(peer != HUB)
            def _():
                pl.semaphore_signal(barrier, inc=1, device_id=(peer, tile), device_id_type=MESH)

        @pl.when(me == HUB)
        def _():
            for k in range(1, GROUP):
                pl.semaphore_signal(barrier, inc=1, device_id=(me, (tile + k) % GROUP), device_id_type=MESH)

    rows = row_index()
    half_tokens = tok_in.shape[1] // HALVES
    to_chunks = one_hot((rows & 3) * half_tokens + (rows >> 3) * 2 + ((rows >> 2) & 1))
    from_chunks = one_hot(((rows % half_tokens) >> 1) * CHUNK + (rows & 1) * 4 + rows // half_tokens)
    before = one_hot((rows + ROWS - jnp.where((rows & 3) == 0, 5, 1)) % ROWS)
    after = one_hot((rows + jnp.where((rows & 3) == 3, 5, 1)) % ROWS)

    def pack(src, dst, h):
        flat = src[:, pl.ds(h * half_tokens, half_tokens), :].reshape(ROWS, channels)
        dst[h] = dot(to_chunks, flat).astype(BF16).reshape(GROUP, CHUNK, channels)

    def exchange_copy(a, src, dst, h, k, cols=slice(None)):
        to = partner_of(me, k)
        return pltpu.make_async_remote_copy(
            src_ref=src.at[h, to, :, cols],
            dst_ref=dst.at[h, me, :, cols],
            send_sem=send_sem.at[a, k],
            recv_sem=recv_sem.at[a, k],
            device_id=(to, tile),
            device_id_type=MESH,
        )

    def arrival(a, src, dst, h, k, cols=slice(None)):
        origin = source_of(me, k)
        return pltpu.make_async_remote_copy(
            src_ref=src.at[h, origin, :, cols],
            dst_ref=dst.at[h, origin, :, cols],
            send_sem=send_sem.at[a, k],
            recv_sem=recv_sem.at[a, k],
            device_id=(origin, tile),
            device_id_type=MESH,
        )

    def send(a, src, dst, h, cols=slice(None)):
        if comm:
            for k in range(GROUP - 1, 0, -1):
                launch(exchange_copy(a, src, dst, h, k, cols))
        dst[h, me, :, cols] = src[h, me, :, cols]

    def receive(a, src, dst, h, cols=slice(None)):
        if comm:
            for k in range(GROUP - 1, 0, -1):
                arrival(a, src, dst, h, k, cols).wait_recv()

    def small_copy(a, src, dst, k, to):
        return pltpu.make_async_remote_copy(
            src_ref=src,
            dst_ref=dst,
            send_sem=small_send.at[a, k],
            recv_sem=small_recv.at[a, k],
            device_id=to,
            device_id_type=MESH,
        )

    step = 256

    def transpose_weight(i):
        loads[2 + i].wait()
        for c in range(0, channels, step):
            wt[i, :, c : c + step] = w[i, c : c + step, :].T

    def local_energy():
        return small_copy(0, esend, erecv.at[me], me, (HUB, tile))

    def hub_energy(k):
        return small_copy(1, hsend, hrecv.at[tile], k, (me, (tile + k) % GROUP))

    def hub_factor(k):
        return small_copy(2, fsend, frecv, k, ((me + k) % GROUP, tile))

    def send_local_energy():
        if comm:

            @pl.when(me != HUB)
            def _():
                local_energy().start()

        @pl.when(me == HUB)
        def _():
            erecv[me] = esend[...]

    def send_hub_energy():
        @pl.when(me == HUB)
        def _():
            if comm:
                for k in range(1, GROUP):
                    peer = (me + k) % GROUP
                    small_copy(0, esend, erecv.at[peer], peer, (peer, tile)).wait_recv()
                pl.semaphore_wait(barrier, GROUP - 1)
            sums = jnp.sum(erecv[...].reshape(ROWS, 128), axis=1, keepdims=True)
            hsend[...] = jnp.broadcast_to(sums, (ROWS, 128)).T[:8]
            hrecv[tile] = hsend[...]
            if comm:
                for k in range(1, GROUP):
                    hub_energy(k).start()

    def send_factor():
        @pl.when(me == HUB)
        def _():
            if comm:
                for k in range(1, GROUP):
                    peer = (tile + GROUP - k) % GROUP
                    small_copy(1, hsend, hrecv.at[peer], k, (me, peer)).wait_recv()
            energy = hrecv[0]
            for t in range(1, GROUP):
                energy = energy + hrecv[t]
            count = tok_in.shape[1] * GROUP * channels
            fsend[...] = lax.rsqrt(energy / count + 1e-06)
            frecv[...] = fsend[...]
            if comm:
                for k in range(1, GROUP):
                    hub_factor(k).start()

    def receive_factor():
        if comm:

            @pl.when(me != HUB)
            def _():
                small_copy(2, fsend, frecv, (me + GROUP - HUB) % GROUP, (HUB, tile)).wait_recv()
                local_energy().wait_send()

            @pl.when(me == HUB)
            def _():
                for k in range(1, GROUP):
                    hub_energy(k).wait_send()
                    hub_factor(k).wait_send()

    loads[0].wait()
    pack(tok_in, tsend, 0)
    loads[1].wait()
    parts = []
    for f in range(cot_in.shape[0]):
        frame = cot_in[f].astype(F32)
        parts.append(jnp.sum(frame * frame, axis=0, keepdims=True))
    squares = jnp.concatenate(parts + parts, axis=0)
    lanes_sum = squares[:, :128]
    for c in range(128, channels, 128):
        lanes_sum = lanes_sum + squares[:, c : c + 128]
    esend[...] = lanes_sum
    for load in loads[2:]:
        load.start()
    if comm:

        @pl.when(me != HUB)
        def _():
            pl.semaphore_wait(barrier, GROUP - 1)

        @pl.when(me == HUB - 1)
        def _():
            pl.semaphore_signal(go_sem, inc=1, device_id=(HUB, tile), device_id_type=MESH)

        @pl.when(me == HUB)
        def _():
            pl.semaphore_wait(go_sem, 1)

    send_local_energy()
    send_hub_energy()
    send(0, tsend, trecv, 0)
    pack(tok_in, tsend, 1)
    send(1, tsend, trecv, 1)
    pack(cot_in, csend, 0)
    pack(cot_in, csend, 1)
    transpose_weight(0)
    transpose_weight(1)
    transpose_weight(2)
    send(2, csend, crecv, 0)

    same_token = ((row_index() >> 2) & 1) == ((lax.broadcasted_iota(jnp.int32, (ROWS, ROWS), 1) >> 2) & 1)
    closed = jnp.where(same_token, 0.0, -1e30).astype(F32)
    closed = jnp.concatenate([closed, closed], axis=1)
    for h in range(HALVES):
        receive(h, tsend, trecv, h)
        for c in range(0, channels, step):
            cols = slice(c, c + step)
            x = trecv[h, :, :, cols].reshape(ROWS, step)
            prev, succ, here = dot(before, x), dot(after, x), x.astype(F32)
            mixed = taps_ref[0:1, cols] * prev + taps_ref[1:2, cols] * here + taps_ref[2:3, cols] * succ
            hid[h, :, cols] = (here + mixed + bias_ref[cols].reshape(1, step)).astype(BF16)
        for i in range(3):
            for c in range(0, channels, step):
                cols = slice(c, c + step)
                block = dot(hid[h], w[i, :, cols])
                if i == 0:
                    block = block * SCALE
                qkv[i, h, :, cols] = block.astype(BF16)
        for m in range(channels // PAIR):
            cols = slice(m * PAIR, (m + 1) * PAIR)
            qs = stacked(qkv[0, h, :, cols])
            qs_all[h, m] = qs
            scores = dot(qkv[1, h, :, cols], qs, ((1,), (1,))) + closed
            expo = jnp.exp(scores - jnp.max(scores, axis=0, keepdims=True))
            probs[h, m] = expo / jnp.sum(expo, axis=0, keepdims=True)
        if h == 0:
            send_factor()
            send(3, csend, crecv, 1)

    for h in range(HALVES):
        if h == 0:
            receive_factor()
            factor = jnp.broadcast_to(frecv[0:1], (ROWS, 128)).T
        receive(2 + h, csend, crecv, h)
        for m in range(channels // PAIR):
            cols = slice(m * PAIR, (m + 1) * PAIR)
            grad_out = (crecv[h, :, :, cols].reshape(ROWS, PAIR).astype(F32) * factor).astype(BF16)
            gs = stacked(grad_out)
            grad_prob = dot(qkv[2, h, :, cols], gs, ((1,), (1,)))
            prob = probs[h, m]
            low = prob.astype(BF16)
            delta = jnp.sum(low.astype(F32) * grad_prob, axis=0, keepdims=True)
            grad_scores = (prob * (grad_prob - delta)).astype(BF16)
            grads[2, h, :, cols] = dot(low, gs).astype(BF16)
            grads[1, h, :, cols] = dot(grad_scores, qs_all[h, m]).astype(BF16)
            both = dot(grad_scores, qkv[1, h, :, cols], ((0,), (0,)))
            lanes = lax.broadcasted_iota(jnp.int32, (ROWS, PAIR), 1)
            grads[0, h, :, cols] = (jnp.where(lanes < HEAD_DIM, both[:ROWS], both[ROWS:]) * SCALE).astype(BF16)
        for c in range(0, channels, step):
            cols = slice(c, c + step)
            total = dot(grads[0, h], wt[0, :, cols])
            total = total + dot(grads[1, h], wt[1, :, cols])
            total = total + dot(grads[2, h], wt[2, :, cols])
            x = total.astype(BF16)
            prev, succ, here = dot(before, x), dot(after, x), x.astype(F32)
            back = here + taps_ref[0:1, cols] * succ + taps_ref[1:2, cols] * here + taps_ref[2:3, cols] * prev
            gsend[h, :, :, cols] = back.astype(BF16).reshape(GROUP, CHUNK, step)
            for part, (first, last) in enumerate(SPLITS):
                if c + step == last:
                    send(4 + 2 * h + part, gsend, grecv, h, slice(first, last))

    for h in range(HALVES):
        for part, (first, last) in enumerate(SPLITS):
            cols = slice(first, last)
            receive(4 + 2 * h + part, gsend, grecv, h, cols)
            flat = dot(from_chunks, grecv[h, :, :, cols].reshape(ROWS, last - first)).astype(BF16)
            toks = pl.ds(h * half_tokens, half_tokens)
            out_ref[:, toks, cols] = flat.reshape(out_ref.shape[0], half_tokens, last - first)

    drain()


def shards(comm, tokens, cotangent, w_query, w_key, w_value, conv_taps, conv_bias):
    frames, toks, channels = tokens.shape
    pairs = channels // PAIR
    exchange = pltpu.VMEM((HALVES, GROUP, CHUNK, channels), BF16)
    hbm, vmem = pl.BlockSpec(memory_space=pl.ANY), pl.BlockSpec(memory_space=pltpu.VMEM)
    return pl.pallas_call(
        functools.partial(kernel, comm),
        out_shape=pltpu.VMEM((frames, toks, channels), BF16),
        in_specs=[hbm, hbm, hbm, hbm, hbm, vmem, vmem],
        out_specs=vmem,
        scratch_shapes=[
            pltpu.VMEM((frames, toks, channels), BF16),
            pltpu.VMEM((frames, toks, channels), BF16),
            pltpu.VMEM((3, channels, channels), BF16),
            pltpu.VMEM((3, channels, channels), BF16),
            exchange,
            exchange,
            exchange,
            exchange,
            exchange,
            exchange,
            pltpu.VMEM((8, 128), F32),
            pltpu.VMEM((GROUP, 8, 128), F32),
            pltpu.VMEM((8, 128), F32),
            pltpu.VMEM((GROUP, 8, 128), F32),
            pltpu.VMEM((8, 128), F32),
            pltpu.VMEM((8, 128), F32),
            pltpu.VMEM((HALVES, ROWS, channels), BF16),
            pltpu.VMEM((3, HALVES, ROWS, channels), BF16),
            pltpu.VMEM((HALVES, pairs, 2 * ROWS, PAIR), BF16),
            pltpu.VMEM((HALVES, pairs, ROWS, 2 * ROWS), F32),
            pltpu.VMEM((3, HALVES, ROWS, channels), BF16),
            pltpu.SemaphoreType.DMA((5,)),
            pltpu.SemaphoreType.DMA((8, GROUP)),
            pltpu.SemaphoreType.DMA((8, GROUP)),
            pltpu.SemaphoreType.DMA((3, GROUP)),
            pltpu.SemaphoreType.DMA((3, GROUP)),
            pltpu.SemaphoreType.REGULAR,
        ],
        compiler_params=pltpu.CompilerParams(
            collective_id=0, has_side_effects=True, vmem_limit_bytes=58 << 20
        ),
    )(tokens, cotangent, w_query, w_key, w_value, conv_taps, conv_bias)


def solution(mesh, comm=True):
    in_specs = (P("orbit", "tile", None), P("orbit", "tile", None), P(), P(), P(), P(), P())
    out_specs = P("orbit", "tile", None)
    return jax.shard_map(
        functools.partial(shards, comm), mesh=mesh, in_specs=in_specs, out_specs=out_specs, check_vma=False
    )
```

time: 57.7 us -> 46.8 us (0.81)
  Pallas kernels: 54.3 us -> 45.8 us
  local copies, waits for them, and re-layouts: 3.26 us -> 0.84 us
    pallas_call x1, Pallas kernels: 54.3 us -> 45.8 us  [shards(): pl.pallas_call(functools.partial(kernel, comm), out_shape=pltpu.VMEM((fra...]
    reshape x1 -> x0, local copies, waits for them, and re-layouts: 1.29 us -> none  [shards(): conv_bias.reshape(1, channels)]
    unnamed x1, local copies, waits for them, and re-layouts: 1.97 us -> 0.84 us
where the time goes in v2:
time: 46.8 us; the launch traced here: 46.7 us
  Pallas kernels  45.8 us (98%)
  local copies, waits for them, and re-layouts  0.84 us (2%)
    pallas_call x1, Pallas kernels, shards(): pl.pallas_call(functools.partial(kernel, comm), out_shape=pltpu.VMEM((fra...  45.8 us

profile of v2, /device:TPU:1, one launch (start us, length us, event | category | flops | bytes accessed | tf_op | source)
XLA Modules:
  0.0 46.7 jit_solution(9963660750034009359)
XLA Ops:
  0.0 45.8 %shard_map.73 = bf16[4,64,1280]{2,1,0:T(8,128)(2,1)S(1)} custom-call(bf16[4,64,1280]{2,1,0:T(8,128)(2,1)} %tokens_hbm.1, bf16[4,64,1280]{2,1,0:T(8,128)(2,1)} %cot_hbm.1, bf16[1280,1280]{1,0:T(8,128)(2,1)} %wq_hbm.1, bf16[1280,1280]{1,0:T(8,128)(2,1)} %wk_hbm.1, bf16[1280,1280]{1,0:T(8,128)(2,1)} %wv_hbm.1, f32[3,1280]{1,0:T(4,128)} %taps_ref.1, f32[1280]{0:T(1024)} %bias_ref.1), custom_call_target="tpu_custom_call" | custom-call | tf_op jit(solution)/shard_map/pallas_call | solution.py:374
  45.8 0.8 %copy.9 = bf16[4,64,1280]{2,1,0:T(8,128)(2,1)} copy(bf16[4,64,1280]{2,1,0:T(8,128)(2,1)S(1)} %shard_map.73) | data formatting | bytes 1310720
